TPU v7x, 32 devices: a whole 2x2x4 slice. The times are simulated.
32 devices in a mesh: dp: 16 (over z, y, x), tensor: 2 (over core).
Axes of the slice: x: 2, y: 2, z: 4, core: 2. Of those that a mesh axis runs over, the one named last changes fastest.
Arguments:
- tokens: bfloat16 [16, 2048, 512], P('dp', 'tensor'), may hold values from -6 to 6
- cotangent: bfloat16 [16, 2048, 512], P('dp', 'tensor'), may hold values from -6 to 6
- span_ids: int32 [16, 8, 256], P('dp'), may hold values from 0 to 1, never falling along the last dimension, each value on 1 to 192 neighbouring positions
- gain_one: float32 [512], replicated, may hold values from 0.25 to 1.75
- w_qkv: bfloat16 [512, 3, 512], P('dp', None, 'tensor'), may hold values from -0.25 to 0.25
- w_out: bfloat16 [512, 512], P('tensor', 'dp'), may hold values from -1 to 1
- b_out: float32 [512], replicated, may hold values from -3 to 3
- gain_two: float32 [512], replicated, may hold values from 0.25 to 1.75
- w_up: bfloat16 [512, 2048], P('dp', 'tensor'), may hold values from -0.25 to 0.25
- b_up: float32 [2048], P('tensor'), may hold values from -3 to 3
- w_down: bfloat16 [2048, 512], P('tensor', 'dp'), may hold values from -0.125 to 0.125
- b_down: float32 [512], replicated, may hold values from -3 to 3
Outputs:
- result: bfloat16 [16, 2048, 512], P('dp', 'tensor')
- d_tokens: bfloat16 [16, 2048, 512], P('dp', 'tensor')
- d_gain_one: float32 [512], replicated
- d_w_qkv: float32 [512, 3, 512], P('dp', None, 'tensor')
- d_w_out: float32 [512, 512], P('tensor', 'dp')
- d_b_out: float32 [512], replicated
- d_gain_two: float32 [512], replicated
- d_w_up: float32 [512, 2048], P('dp', 'tensor')
- d_b_up: float32 [2048], replicated
- d_w_down: float32 [2048, 512], P('tensor', 'dp')
- d_b_down: float32 [512], replicated
Inputs may be any that keep to these rules, and one draw needn't show every extreme that they name: `span_ids`: within each block of 256 positions the span numbers never fall and each of the 2 spans holds 1 to 192 positions.
All inputs are finite; a program needn't handle non-finite values.
Results may differ from a plain program's by a relative error of at most 0.014.
Values may be sent and summed in bfloat16 or wider, within the bound.
A program may use at most 128 MiB of HBM per device.

v0:
```python
import math
import jax
import jax.numpy as jnp
from jax import lax
from jax.sharding import PartitionSpec as P

HD = 64
BLK = 256
SPB = 2
epsilon = 1e-05
masked = -1e30


def normalize(values, gain_vec):
    centre = values - jnp.mean(values, axis=-1, keepdims=True)
    spread = jnp.mean(centre * centre, axis=-1, keepdims=True)
    inverse = lax.rsqrt(spread + epsilon)
    unit_rows = centre * inverse
    return (unit_rows, inverse, unit_rows * gain_vec)


def normalize_back(incoming_grad, unit_rows, inverse, gain_vec):
    scaled = incoming_grad * gain_vec
    mean_one = jnp.mean(scaled, axis=-1, keepdims=True)
    mean_two = jnp.mean(scaled * unit_rows, axis=-1, keepdims=True)
    return (
        inverse * (scaled - mean_one - unit_rows * mean_two),
        jnp.sum(incoming_grad * unit_rows, axis=0),
    )


def pair_rows(values):
    return lax.all_gather(values, "tensor", axis=0, tiled=True)


def pair_sums(term_fn, rows):
    return lax.psum_scatter(
        term_fn(jnp.int32(0), rows * lax.axis_size("tensor")).astype(jnp.bfloat16),
        "tensor",
        scatter_dimension=0,
        tiled=True,
    ).astype(jnp.float32)


def scores(queries, key_rows, key_sum, counts_all, allowed):
    scaling = 1.0 / math.sqrt(queries.shape[-1])
    near_scores = (
        jnp.einsum("bie,bje->bij", queries, key_rows, preferred_element_type=jnp.float32) * scaling
    )
    far_scores = (
        jnp.einsum("bie,ce->bic", queries, key_sum, preferred_element_type=jnp.float32) * scaling
    )
    far_scores = far_scores + jnp.log(counts_all).reshape(-1)
    far_scores = jnp.where(allowed[:, None, :], far_scores, masked)
    return (near_scores, far_scores)


def span_means(key_rows, value_rows, member_low, counts):
    head_size = key_rows.shape[-1]
    key_sum = jnp.einsum("bjm,bje->bme", member_low, key_rows, preferred_element_type=jnp.float32)
    value_sum = jnp.einsum(
        "bjm,bje->bme", member_low, value_rows, preferred_element_type=jnp.float32
    )
    key_sum = (key_sum / counts[:, :, None]).astype(jnp.bfloat16).reshape(-1, head_size)
    value_sum = (value_sum / counts[:, :, None]).astype(jnp.bfloat16).reshape(-1, head_size)
    return (key_sum, value_sum)


def attend(queries, key_rows, value_rows, key_sum, value_sum, counts_all, allowed):
    near_scores, far_scores = scores(queries, key_rows, key_sum, counts_all, allowed)
    largest = jnp.maximum(jnp.max(near_scores, axis=-1), jnp.max(far_scores, axis=-1))
    near_exp = jnp.exp(near_scores - largest[..., None])
    far_exp = jnp.exp(far_scores - largest[..., None])
    denominator = jnp.sum(near_exp, axis=-1) + jnp.sum(far_exp, axis=-1)
    near_prob = (near_exp / denominator[..., None]).astype(jnp.bfloat16)
    far_prob = (far_exp / denominator[..., None]).astype(jnp.bfloat16)
    attended = jnp.einsum("bij,bje->bie", near_prob, value_rows, preferred_element_type=jnp.float32)
    attended = attended + jnp.einsum(
        "bic,ce->bie", far_prob, value_sum, preferred_element_type=jnp.float32
    )
    return (attended.astype(jnp.bfloat16), largest + jnp.log(denominator))


def head_backward(
    queries, key_rows, value_rows, grad_heads, log_total, key_sum, value_sum, counts_all, allowed
):
    scaling = 1.0 / math.sqrt(queries.shape[-1])
    near_scores, far_scores = scores(queries, key_rows, key_sum, counts_all, allowed)
    near_prob = jnp.exp(near_scores - log_total[..., None])
    far_prob = jnp.exp(far_scores - log_total[..., None])
    grad_value = jnp.einsum(
        "bij,bie->bje",
        near_prob.astype(jnp.bfloat16),
        grad_heads,
        preferred_element_type=jnp.float32,
    )
    grad_vsum = jnp.einsum(
        "bic,bie->ce", far_prob.astype(jnp.bfloat16), grad_heads, preferred_element_type=jnp.float32
    )
    near_dprob = jnp.einsum(
        "bie,bje->bij", grad_heads, value_rows, preferred_element_type=jnp.float32
    )
    far_dprob = jnp.einsum("bie,ce->bic", grad_heads, value_sum, preferred_element_type=jnp.float32)
    correction = jnp.sum(near_prob * near_dprob, axis=-1) + jnp.sum(far_prob * far_dprob, axis=-1)
    near_grad = (near_prob * (near_dprob - correction[..., None])).astype(jnp.bfloat16)
    far_grad = (far_prob * (far_dprob - correction[..., None])).astype(jnp.bfloat16)
    grad_query = jnp.einsum("bij,bje->bie", near_grad, key_rows, preferred_element_type=jnp.float32)
    grad_query = (
        grad_query
        + jnp.einsum("bic,ce->bie", far_grad, key_sum, preferred_element_type=jnp.float32)
    ) * scaling
    grad_key = (
        jnp.einsum("bij,bie->bje", near_grad, queries, preferred_element_type=jnp.float32) * scaling
    )
    grad_ksum = (
        jnp.einsum("bic,bie->ce", far_grad, queries, preferred_element_type=jnp.float32) * scaling
    )
    return (grad_query.astype(jnp.bfloat16), grad_key, grad_value, grad_ksum, grad_vsum)


def shards(
    tokens, cotangent, span_ids, gain_one, w_qkv, w_out, b_out, gain_two, w_up, b_up, w_down, b_down
):
    incoming = tokens[0].astype(jnp.float32)
    row_count = incoming.shape[0]
    full_qkv, full_out, full_up, full_down = (
        lax.all_gather(w_qkv, "dp", axis=0, tiled=True),
        lax.all_gather(w_out, "dp", axis=1, tiled=True),
        lax.all_gather(w_up, "dp", axis=0, tiled=True),
        lax.all_gather(w_down, "dp", axis=1, tiled=True),
    )
    unit_one, inverse_one, normed = normalize(incoming, gain_one)
    normed_low = normed.astype(jnp.bfloat16)
    span_all = span_ids[0]
    member_all = (span_all[:, :, None] == jnp.arange(SPB, dtype=jnp.int32)[None, None, :]).astype(
        jnp.float32
    )
    counts_all = jnp.sum(member_all, axis=1)
    total_blocks = span_all.shape[0]
    qkv_whole, out_whole, up_whole, down_whole, bias_whole = (
        full_qkv,
        full_out,
        full_up,
        full_down,
        b_up,
    )
    rows_one = pair_rows(normed_low)
    width = qkv_whole.shape[0]
    qkv_flat = qkv_whole.reshape(width, -1)
    length = rows_one.shape[0]
    blocks = length // BLK
    heads_here = qkv_whole.shape[2] // HD
    projected = jnp.dot(rows_one, qkv_flat, preferred_element_type=jnp.float32).astype(jnp.bfloat16)
    per_head = jnp.moveaxis(projected.reshape(blocks, BLK, 3, heads_here, HD), (2, 3), (0, 1))
    member_low = member_all.astype(jnp.bfloat16)
    allowed = jnp.arange(blocks)[:, None] > (jnp.arange(total_blocks * SPB) // SPB)[None, :]
    key_sums, value_sums = lax.map(
        lambda pieces: span_means(pieces[0], pieces[1], member_low, counts_all),
        (per_head[1], per_head[2]),
    )

    def forward_head(pieces):
        return attend(pieces[0], pieces[1], pieces[2], pieces[3], pieces[4], counts_all, allowed)

    attended, log_total = lax.map(
        forward_head, (per_head[0], per_head[1], per_head[2], key_sums, value_sums)
    )
    attended_flat = jnp.moveaxis(attended, 0, 2).reshape(length, -1)

    def project_attn(offset, amount):
        return jnp.dot(attended_flat, out_whole, preferred_element_type=jnp.float32)

    attn_total = pair_sums(project_attn, row_count)
    middle = incoming + (attn_total + b_out)
    unit_two, inverse_two, normed_two = normalize(middle, gain_two)
    rows_two = pair_rows(normed_two.astype(jnp.bfloat16))
    before_gelu = jnp.dot(rows_two, up_whole, preferred_element_type=jnp.float32) + bias_whole
    activated, gelu_pull = jax.vjp(jax.nn.gelu, before_gelu)
    hidden = activated.astype(jnp.bfloat16)

    def project_mlp(offset, amount):
        return jnp.dot(hidden, down_whole, preferred_element_type=jnp.float32)

    mlp_total = pair_sums(project_mlp, row_count)
    output = middle + (mlp_total + b_down)
    grad_rows = cotangent[0]
    grad_output = grad_rows.astype(jnp.float32)
    full_grad = pair_rows(grad_rows)
    grad_down = jnp.einsum("sf,sd->fd", hidden, full_grad, preferred_element_type=jnp.float32)
    grad_hidden = jnp.einsum("sd,fd->sf", full_grad, down_whole, preferred_element_type=jnp.float32)
    grad_inner = gelu_pull(grad_hidden)[0].astype(jnp.bfloat16)
    bias_up = jnp.sum(grad_inner, axis=0, dtype=jnp.float32)
    grad_up = jnp.einsum("sd,sf->df", rows_two, grad_inner, preferred_element_type=jnp.float32)

    def back_mlp_rows(offset, amount):
        return jnp.einsum("sf,df->sd", grad_inner, up_whole, preferred_element_type=jnp.float32)

    grad_second = pair_sums(back_mlp_rows, row_count)
    grad_norm_two, gain_two_part = normalize_back(grad_second, unit_two, inverse_two, gain_two)
    grad_mid = grad_output + grad_norm_two
    grad_branch = grad_mid.astype(jnp.bfloat16)
    full_branch = pair_rows(grad_branch)
    grad_wout = jnp.einsum(
        "sh,sd->hd", attended_flat, full_branch, preferred_element_type=jnp.float32
    )
    grad_attended = jnp.einsum(
        "sd,hd->sh", full_branch, out_whole, preferred_element_type=jnp.float32
    ).astype(jnp.bfloat16)
    grad_heads = jnp.moveaxis(grad_attended.reshape(blocks, BLK, heads_here, HD), 2, 0)

    def backward_head(pieces):
        return head_backward(
            pieces[0],
            pieces[1],
            pieces[2],
            pieces[3],
            pieces[4],
            pieces[5],
            pieces[6],
            counts_all,
            allowed,
        )

    grad_query, grad_key, grad_value, grad_ksums, grad_vsums = lax.map(
        backward_head,
        (per_head[0], per_head[1], per_head[2], grad_heads, log_total, key_sums, value_sums),
    )
    share_key = grad_ksums.reshape(heads_here, blocks, SPB, HD) / counts_all[None, :, :, None]
    share_value = grad_vsums.reshape(heads_here, blocks, SPB, HD) / counts_all[None, :, :, None]
    grad_key = (grad_key + jnp.einsum("bjm,hbme->hbje", member_all, share_key)).astype(jnp.bfloat16)
    grad_value = (grad_value + jnp.einsum("bjm,hbme->hbje", member_all, share_value)).astype(
        jnp.bfloat16
    )
    grad_projected = jnp.moveaxis(
        jnp.stack((grad_query, grad_key, grad_value), axis=0), (0, 1), (2, 3)
    ).reshape(length, -1)
    grad_qkv = jnp.einsum(
        "sd,sc->dc", rows_one, grad_projected, preferred_element_type=jnp.float32
    ).reshape(qkv_whole.shape)

    def back_attn_rows(offset, amount):
        return jnp.einsum("sc,dc->sd", grad_projected, qkv_flat, preferred_element_type=jnp.float32)

    grad_first = pair_sums(back_attn_rows, row_count)
    grad_norm_one, gain_one_part = normalize_back(grad_first, unit_one, inverse_one, gain_one)
    grad_input = grad_mid + grad_norm_one
    half_width = bias_up.shape[0]
    bias_up_full = lax.dynamic_update_slice(
        jnp.zeros((half_width * lax.axis_size("tensor"),), jnp.float32),
        bias_up,
        (lax.axis_index("tensor") * half_width,),
    )
    totals = lax.psum(
        (
            gain_one_part,
            gain_two_part,
            jnp.sum(grad_branch, axis=0, dtype=jnp.float32),
            jnp.sum(grad_output, axis=0),
            bias_up_full,
        ),
        ("dp", "tensor"),
    )
    grad_qkv, grad_wout, grad_up, grad_down = (
        lax.psum_scatter(grad_qkv, "dp", scatter_dimension=0, tiled=True),
        lax.psum_scatter(grad_wout, "dp", scatter_dimension=1, tiled=True),
        lax.psum_scatter(grad_up, "dp", scatter_dimension=0, tiled=True),
        lax.psum_scatter(grad_down, "dp", scatter_dimension=1, tiled=True),
    )
    factor = 1.0 / math.sqrt(lax.axis_size("dp") * lax.axis_size("tensor") * row_count)
    return (
        output.astype(jnp.bfloat16)[None],
        grad_input.astype(jnp.bfloat16)[None],
        totals[0] * factor,
        grad_qkv * factor,
        grad_wout * factor,
        totals[2] * factor,
        totals[1] * factor,
        grad_up * factor,
        totals[4] * factor,
        grad_down * factor,
        totals[3] * factor,
    )


def solution(mesh):
    in_specs = (
        P("dp", "tensor", None),
        P("dp", "tensor", None),
        P("dp", None, None),
        P(),
        P("dp", None, "tensor"),
        P("tensor", "dp"),
        P(),
        P(),
        P("dp", "tensor"),
        P("tensor"),
        P("tensor", "dp"),
        P(),
    )
    out_specs = (
        P("dp", "tensor", None),
        P("dp", "tensor", None),
        P(),
        P("dp", None, "tensor"),
        P("tensor", "dp"),
        P(),
        P(),
        P("dp", "tensor"),
        P(),
        P("tensor", "dp"),
        P(),
    )
    return jax.shard_map(shards, mesh=mesh, in_specs=in_specs, out_specs=out_specs, check_vma=False)
```

profile of v0, /device:TPU:0, one launch (start us, length us, event | category | flops | bytes accessed | tf_op | source)
XLA Modules:
  0.0 714.1 jit_solution(7615604891802510770)
XLA Ops:
  13.1 47.0 %all_gather.25 = bf16[512,3,256]{2,0,1:T(8,128)(2,1)S(1)} all-gather(bf16[32,3,256]{2,0,1:T(8,128)(2,1)S(1)} %copy-done.14), channel_id=1, replica_groups=mesh['dp'=16,'tensor'=2] {'dp'}, dimensions={0}, use_global_device_ids=true | all-gather | bytes 835584 | tf_op jit(solution)/shard_map/all_gather | solution.py:127
  60.4 36.9 %all_gather.26 = bf16[256,512]{0,1:T(8,128)(2,1)S(1)} all-gather(bf16[256,32]{0,1:T(8,128)(2,1)S(1)} %copy-done.18), channel_id=1, replica_groups=mesh['dp'=16,'tensor'=2] {'dp'}, dimensions={1}, use_global_device_ids=true | all-gather | bytes 278528 | tf_op jit(solution)/shard_map/all_gather | solution.py:128
  97.3 5.1 convolution_convert_fusion
  102.4 4.7 copy.64
  115.9 14.6 %while.50 = (s32[]{:T(128)}, bf16[4,8,256,64]{2,3,1,0:T(8,128)(2,1)}, f32[4,8,256]{2,1,0:T(8,128)S(1)}, bf16[4,8,256,64]{2,3,1,0:T(8,128)(2,1)S(1)}, bf16[4,8,25...) while((s32[]{:T(128)}, ...), condition=%wide.region_10.11_spmd.clone, body=%wide.region_5.10_spmd.clone.sunk | while | flops 147880064 | bytes 9204541 | solution.py:165
  136.7 6.9 reduce-scatter.9.cloned.1.call-done
  149.1 43.8 %all-gather.12.cloned.1.call-done = bf16[512,1024]{1,0:T(8,128)(2,1)} async-done(((bf16[32,1024]{1,0:T(8,128)(2,1)}), bf16[512,1024]{1,0:T(8,128)(2,1)}) %all-gather.12.cloned.1.call-update) | async-done | bytes 1048592 | tf_op jit(solution)/shard_map/all_gather | solution.py:129
  192.9 11.4 %all-gather.10.cloned.1.call-done = bf16[2048,512]{1,0:T(8,128)(2,1)} async-done(((bf16[1024,512]{1,0:T(8,128)(2,1)}), bf16[2048,512]{1,0:T(8,128)(2,1)}) %all-gather.10.cloned.1.call-update) | async-done | bytes 2097168 | tf_op jit(solution)/shard_map/all_gather | solution.py:33
  204.3 10.5 %multiply_convert_fusion.2 = (bf16[2048,1024]{1,0:T(8,128)(2,1)}, f32[2048,1024]{1,0:T(8,128)}) fusion(f32[1024]{0:T(1024)S(1)} %copy-done.22, bf16[2048,512]{1,0:T(8,128)(2,1)} %all-gather.10.cloned.1.call-done, bf16[512,1024]{1,0:T(8,128)(2,1)} %all-gather.12.cloned.1.call-done), kind=kOutput, calls=%fused_computation.129 | convolution fusion | flops 2168455168 | bytes 15732736 | tf_op jit(solution)/shard_map/dot_general | solution.py:177
  214.8 49.1 %all-gather.14.cloned.1.call-done = bf16[1024,512]{0,1:T(8,128)(2,1)} async-done(((bf16[1024,32]{0,1:T(8,128)(2,1)}), bf16[1024,512]{0,1:T(8,128)(2,1)}) %all-gather.14.cloned.1.call-update) | async-done | bytes 1048592 | tf_op jit(solution)/shard_map/all_gather | solution.py:130
  263.9 11.0 %all-gather.18.cloned.1.call-done = bf16[1,2048,512]{2,1,0:T(8,128)(2,1)} async-done(((bf16[1,1024,512]{2,1,0:T(8,128)(2,1)}), bf16[1,2048,512]{2,1,0:T(8,128)(2,1)}) %all-gather.18.cloned.1.call-update) | async-done | bytes 2097168 | tf_op jit(solution)/shard_map/all_gather | solution.py:33
  274.9 10.2 %convert_reduce_fusion = (f32[1024]{0:T(1024)S(1)}, bf16[2048,1024]{1,0:T(8,128)(2,1)S(1)}) fusion(f32[2048,1024]{1,0:T(8,128)} %get-tuple-element.582, f32[1024]{0:T(1024)S(1)} %copy-done.22, bf16[1024,512]{0,1:T(8,128)(2,1)} %all-gather.14.cloned.1.call-done, bf16[1,2048,512]{2,1,0:T(8,128)(2,1)} %all-gather.18.cloned.1.call-done), kind=kOutput, calls=%fused_computation.128 | convolution fusion | flops 2195717120 | bytes 15736832 | tf_op jit(solution)/shard_map/sd,fd->sf/dot_general | solution.py:190
  291.1 6.2 convolution_convert_fusion.2
  304.7 10.0 %reduce-scatter.11.cloned.1.call-done = bf16[1024,512]{1,0:T(8,128)(2,1)} async-done(((bf16[2048,512]{1,0:T(8,128)(2,1)}), bf16[1024,512]{1,0:T(8,128)(2,1)}) %reduce-scatter.11.cloned.1.call-update) | async-done | bytes 1048592 | tf_op jit(solution)/shard_map/reduce_scatter | solution.py:37
  319.0 6.6 fusion.131
  325.7 7.2 %fusion.155 = f32[512,1024]{1,0:T(8,128)} fusion(bf16[2048,512]{1,0:T(8,128)(2,1)} %all-gather.10.cloned.1.call-done, bf16[2048,1024]{1,0:T(8,128)(2,1)} %copy-done.25), kind=kOutput, calls=%fused_computation.228 | convolution fusion | flops 2147483648 | bytes 8388608 | tf_op jit(solution)/shard_map/sd,sf->df/dot_general | solution.py:193
  341.4 32.6 %while.51 = (s32[]{:T(128)}, bf16[4,8,256,64]{2,3,0,1:T(8,128)(2,1)}, f32[4,8,256,64]{2,3,0,1:T(8,128)}, f32[4,8,256,64]{2,3,0,1:T(8,128)}, f32[4,16,64]{2,1,0:T...) while((s32[]{:T(128)}, ...), condition=%wide.region_21.22_spmd.clone, body=%wide.region_18.21_spmd.clone.sunk | while | flops 361561216 | bytes 22604664 | solution.py:224
  390.9 5.0 convolution_convert_fusion.4
  397.7 17.2 %reduce-scatter.23.cloned.1.call-done = f32[1024,32]{0,1:T(8,128)} async-done(((f32[1024,512]{0,1:T(8,128)}), f32[1024,32]{0,1:T(8,128)}) %reduce-scatter.23.cloned.1.call-update) | async-done | bytes 131088 | tf_op jit(solution)/shard_map/reduce_scatter | solution.py:267
  416.5 78.2 %reduce-scatter.21.cloned.1.call-done = f32[32,1024]{1,0:T(8,128)} async-done(((f32[512,1024]{1,0:T(8,128)}), f32[32,1024]{1,0:T(8,128)}) %reduce-scatter.21.cloned.1.call-update) | async-done | bytes 131088 | tf_op jit(solution)/shard_map/reduce_scatter | solution.py:266
  496.2 74.7 %reduce-scatter.19.cloned.1.call-done = f32[256,32]{0,1:T(8,128)} async-done(((f32[256,512]{0,1:T(8,128)}), f32[256,32]{0,1:T(8,128)}) %reduce-scatter.19.cloned.1.call-update) | async-done | bytes 32784 | tf_op jit(solution)/shard_map/reduce_scatter | solution.py:265
  572.3 76.1 %reduce-scatter.17.cloned.1.call-done = f32[32,3,256]{2,0,1:T(8,128)} async-done(((f32[512,3,256]{2,0,1:T(8,128)}), f32[32,3,256]{2,0,1:T(8,128)}) %reduce-scatter.17.cloned.1.call-update) | async-done | bytes 98320 | tf_op jit(solution)/shard_map/reduce_scatter | solution.py:264
  650.0 7.2 %reduce-scatter.15.cloned.1.call-done = bf16[1024,512]{1,0:T(8,128)(2,1)} async-done(((bf16[2048,512]{1,0:T(8,128)(2,1)}), bf16[1024,512]{1,0:T(8,128)(2,1)}) %reduce-scatter.15.cloned.1.call-update) | async-done | bytes 1048592 | tf_op jit(solution)/shard_map/reduce_scatter | solution.py:37
  659.8 40.7 %all-reduce = (f32[512]{0:T(512)S(1)}, f32[512]{0:T(512)S(1)}, f32[512]{0:T(512)S(1)}, f32[2048]{0:T(1024)S(1)}, f32[512]{0:T(512)S(1)}) all-reduce(f32[512]{0:T(512)S(1)} %get-tuple-element.489, f32[512]{0:T(512)S(1)} %get-tuple-element.564, f32[512]{0:T(512)S(1)} %get-tuple-element.487, ...), channel_id=1, replica_groups=mesh['dp'=16,'tensor'=2] {'dp','tensor'}, use_global_device_ids=true, to_apply=%region_26.27 | all-reduce | flops 4096 | bytes 32768 | tf_op jit(solution)/shard_map/psum | solution.py:253
  (258 shorter events, 133.1 us)
Async XLA Ops:
  8.0 89.3 %all-gather.8.cloned.1.call-start = ((), (), s32[]{:S(2)}) async-start(), calls=%async_computation.8 | async-start | bytes 3145728 | tf_op jit(solution)/shard_map/all_gather | solution.py:33
  12.8 47.6 %copy-start.18 = (bf16[256,32]{0,1:T(8,128)(2,1)S(1)}, bf16[256,32]{0,1:T(8,128)(2,1)}, u32[]{:S(2)}) copy-start(bf16[256,32]{0,1:T(8,128)(2,1)} %param.23) | copy-start | bytes 49156
  12.8 130.9 %reduce-scatter.9.cloned.1.call-start = ((), (), s32[]{:S(2)}) async-start(), calls=%async_computation.9 | async-start | bytes 3145728 | tf_op jit(solution)/shard_map/reduce_scatter | solution.py:37
  60.4 42.1 %copy-start.10 = (bf16[512,3,256]{0,2,1:T(8,128)(2,1)}, bf16[512,3,256]{0,2,1:T(8,128)(2,1)S(1)}, u32[]{:S(2)}) copy-start(bf16[512,3,256]{0,2,1:T(8,128)(2,1)S(1)} %copy.63) | copy-start | bytes 2359300
  133.9 9.7 %copy-start.13 = (f32[512]{0:T(512)S(1)}, f32[512]{0:T(512)}, u32[]{:S(2)}) copy-start(f32[512]{0:T(512)} %param.24) | copy-start | bytes 6148
  136.1 56.8 %all-gather.12.cloned.1.call-start = ((), (), s32[]{:S(2)}) async-start(), calls=%async_computation.11 | async-start | bytes 1114112 | tf_op jit(solution)/shard_map/all_gather | solution.py:129
  136.7 9.4 %copy-start.17 = (f32[512]{0:T(512)S(1)}, f32[512]{0:T(512)}, u32[]{:S(2)}) copy-start(f32[512]{0:T(512)} %param.25) | copy-start | bytes 6148
  136.7 67.6 %all-gather.10.cloned.1.call-start = ((), (), s32[]{:S(2)}) async-start(), calls=%async_computation.10 | async-start | bytes 3145728 | tf_op jit(solution)/shard_map/all_gather | solution.py:33
  146.1 58.2 %copy-start.22 = (f32[1024]{0:T(1024)S(1)}, f32[1024]{0:T(1024)}, u32[]{:S(2)}) copy-start(f32[1024]{0:T(1024)} %param.27) | copy-start | bytes 12292
  147.6 116.3 %all-gather.14.cloned.1.call-start = ((), (), s32[]{:S(2)}) async-start(), calls=%async_computation.12 | async-start | bytes 1114112 | tf_op jit(solution)/shard_map/all_gather | solution.py:130
  148.2 126.7 %all-gather.18.cloned.1.call-start = ((), (), s32[]{:S(2)}) async-start(), calls=%async_computation.21 | async-start | bytes 3145728 | tf_op jit(solution)/shard_map/all_gather | solution.py:33
  148.9 152.9 %reduce-scatter.13.cloned.1.call-start = ((), (), s32[]{:S(2)}) async-start(), calls=%async_computation.14 | async-start | bytes 3145728 | tf_op jit(solution)/shard_map/reduce_scatter | solution.py:37
  274.9 12.1 %copy-start.21 = (bf16[512,1024]{1,0:T(8,128)(2,1)S(1)}, bf16[512,1024]{1,0:T(8,128)(2,1)}, u32[]{:S(2)}) copy-start(bf16[512,1024]{1,0:T(8,128)(2,1)} %all-gather.12.cloned.1.call-done) | copy-start | bytes 3145732
  290.9 23.9 %reduce-scatter.11.cloned.1.call-start = ((), (), s32[]{:S(2)}) async-start(), calls=%async_computation.13 | async-start | bytes 3145728 | tf_op jit(solution)/shard_map/reduce_scatter | solution.py:37
  297.3 17.4 %copy-start.19 = (f32[512]{0:T(512)S(1)}, f32[512]{0:T(512)}, u32[]{:S(2)}) copy-start(f32[512]{0:T(512)} %param.29) | copy-start | bytes 6148
  297.4 35.9 %all-gather.16.cloned.1.call-start = ((), (), s32[]{:S(2)}) async-start(), calls=%async_computation.15 | async-start | bytes 3145728 | tf_op jit(solution)/shard_map/all_gather | solution.py:33
  318.9 95.9 %reduce-scatter.23.cloned.1.call-start = ((), (), s32[]{:S(2)}) async-start(), calls=%async_computation.20 | async-start | bytes 2228224 | tf_op jit(solution)/shard_map/reduce_scatter | solution.py:267
  325.6 169.1 %reduce-scatter.21.cloned.1.call-start = ((), (), s32[]{:S(2)}) async-start(), calls=%async_computation.19 | async-start | bytes 2228224 | tf_op jit(solution)/shard_map/reduce_scatter | solution.py:266
  332.9 238.1 %reduce-scatter.19.cloned.1.call-start = ((), (), s32[]{:S(2)}) async-start(), calls=%async_computation.18 | async-start | bytes 557056 | tf_op jit(solution)/shard_map/reduce_scatter | solution.py:265
  336.5 4.9 copy-start.15
  336.5 4.9 copy-start.24
  377.7 270.8 %reduce-scatter.17.cloned.1.call-start = ((), (), s32[]{:S(2)}) async-start(), calls=%async_computation.17 | async-start | bytes 1671168 | tf_op jit(solution)/shard_map/reduce_scatter | solution.py:264
  390.6 266.6 %reduce-scatter.15.cloned.1.call-start = ((), (), s32[]{:S(2)}) async-start(), calls=%async_computation.16 | async-start | bytes 3145728 | tf_op jit(solution)/shard_map/reduce_scatter | solution.py:37
  657.2 46.3 %copy-start.6 = (bf16[1024,512]{1,0:T(8,128)(2,1)S(1)}, bf16[1024,512]{1,0:T(8,128)(2,1)}, u32[]{:S(2)}) copy-start(bf16[1024,512]{1,0:T(8,128)(2,1)} %reduce-scatter.15.cloned.1.call-done) | copy-start | bytes 3145732
  (16 other events, 40.4 us)
Sparse Core Ops, SparseCore 0:
  12.9 13.2 all-gather.7
  136.2 7.4 reduce-scatter.8
  291.0 10.8 reduce-scatter.12
  303.9 10.7 reduce-scatter.10
Sparse Core Ops, SparseCore 1:
  139.7 53.1 all-gather.11
  195.0 9.3 all-gather.9
  207.3 56.5 all-gather.13
  265.6 9.3 all-gather.17
  319.0 11.6 all-gather.15
  333.1 81.7 reduce-scatter.22
  417.1 77.5 reduce-scatter.20
  497.4 73.5 reduce-scatter.18
  573.1 75.3 reduce-scatter.16
  650.8 6.3 reduce-scatter.14
where the time goes:
time: 723 us; the launch traced here: 714 us
  waiting for transfers between devices  392 us (54%)
  blocking collectives  125 us (17%)
  matrix products  112 us (15%)
  other arithmetic  34.3 us (5%)
  local copies, waits for them, and re-layouts  32.8 us (5%)
  between operations  16.3 us (2%)
    reduce_scatter x1, waiting for transfers between devices, shards(): lax.psum_scatter(grad_up, 'dp', scatter_dimension=0, tiled=True)  78.2 us
    reduce_scatter x1, waiting for transfers between devices, shards(): lax.psum_scatter(grad_qkv, 'dp', scatter_dimension=0, tiled=True)  76.1 us
    reduce_scatter x1, waiting for transfers between devices, shards(): lax.psum_scatter(grad_wout, 'dp', scatter_dimension=1, tiled=True)  74.7 us
    all_gather x1, waiting for transfers between devices, shards(): lax.all_gather(w_down, 'dp', axis=1, tiled=True)  49.1 us
    all_gather x1, blocking collectives, shards(): lax.all_gather(w_qkv, 'dp', axis=0, tiled=True)  47 us
    all_gather x1, waiting for transfers between devices, shards(): lax.all_gather(w_up, 'dp', axis=0, tiled=True)  43.8 us
    psum x1, blocking collectives, shards(): lax.psum((gain_one_part, gain_two_part, jnp.sum(grad_branch, axis=0, dtyp...  40.7 us
    all_gather x1, blocking collectives, shards(): lax.all_gather(w_out, 'dp', axis=1, tiled=True)  36.9 us
  transfers between devices with their start and end apart: 14, of which 12 were waited for; matrix products, arithmetic and copies ran while one was open for 15% of the time, Pallas kernels for 0%

commit v1 on v0

--- a/solution.py
+++ b/solution.py
@@ -250,16 +250,15 @@
         bias_up,
         (lax.axis_index("tensor") * half_width,),
     )
-    totals = lax.psum(
-        (
-            gain_one_part,
-            gain_two_part,
-            jnp.sum(grad_branch, axis=0, dtype=jnp.float32),
-            jnp.sum(grad_output, axis=0),
-            bias_up_full,
-        ),
-        ("dp", "tensor"),
-    )
+    totals = (
+        gain_one_part,
+        gain_two_part,
+        jnp.sum(grad_branch, axis=0, dtype=jnp.float32),
+        jnp.sum(grad_output, axis=0),
+        bias_up_full,
+    )
+    for to_i in ("tensor", "dp"):
+        totals = lax.psum(totals, axis_name=to_i)
     grad_qkv, grad_wout, grad_up, grad_down = (
         lax.psum_scatter(grad_qkv, "dp", scatter_dimension=0, tiled=True),
         lax.psum_scatter(grad_wout, "dp", scatter_dimension=1, tiled=True),

time: 723 us -> 763 us (1.055)
  blocking collectives: 125 us -> 164 us
    psum x1 -> x2, blocking collectives: 40.7 us -> 80.4 us  [shards(): totals = lax.psum(totals, axis_name=to_i)]
  transfers between devices with their start and end apart: 14 -> 14, of which waited for: 12 -> 12; matrix products, arithmetic and copies ran while one was open for 15% -> 14% of each run, Pallas kernels for 0% -> 0%
where the time goes in v1:
time: 763 us; the launch traced here: 754 us
  waiting for transfers between devices  392 us (51%)
  blocking collectives  164 us (21%)
  matrix products  112 us (15%)
  other arithmetic  34.3 us (4%)
  local copies, waits for them, and re-layouts  32.8 us (4%)
  between operations  16.3 us (2%)
    psum x2, blocking collectives, shards(): totals = lax.psum(totals, axis_name=to_i)  80.4 us
    reduce_scatter x1, waiting for transfers between devices, shards(): lax.psum_scatter(grad_up, 'dp', scatter_dimension=0, tiled=True)  78.2 us
    reduce_scatter x1, waiting for transfers between devices, shards(): lax.psum_scatter(grad_qkv, 'dp', scatter_dimension=0, tiled=True)  76.1 us
    reduce_scatter x1, waiting for transfers between devices, shards(): lax.psum_scatter(grad_wout, 'dp', scatter_dimension=1, tiled=True)  74.7 us
    all_gather x1, waiting for transfers between devices, shards(): lax.all_gather(w_down, 'dp', axis=1, tiled=True)  49.1 us
    all_gather x1, blocking collectives, shards(): lax.all_gather(w_qkv, 'dp', axis=0, tiled=True)  47 us
    all_gather x1, waiting for transfers between devices, shards(): lax.all_gather(w_up, 'dp', axis=0, tiled=True)  43.8 us
    all_gather x1, blocking collectives, shards(): lax.all_gather(w_out, 'dp', axis=1, tiled=True)  36.9 us
  transfers between devices with their start and end apart: 14, of which 12 were waited for; matrix products, arithmetic and copies ran while one was open for 14% of the time, Pallas kernels for 0%

profile of v1, /device:TPU:0, one launch (start us, length us, event | category | flops | bytes accessed | tf_op | source)
XLA Modules:
  0.0 753.8 jit_solution(16592284424386134208)
XLA Ops:
  13.1 47.0 %all_gather.25 = bf16[512,3,256]{2,0,1:T(8,128)(2,1)S(1)} all-gather(bf16[32,3,256]{2,0,1:T(8,128)(2,1)S(1)} %copy-done.14), channel_id=1, replica_groups=mesh['dp'=16,'tensor'=2] {'dp'}, dimensions={0}, use_global_device_ids=true | all-gather | bytes 835584 | tf_op jit(solution)/shard_map/all_gather | solution.py:127
  60.4 36.9 %all_gather.26 = bf16[256,512]{0,1:T(8,128)(2,1)S(1)} all-gather(bf16[256,32]{0,1:T(8,128)(2,1)S(1)} %copy-done.18), channel_id=1, replica_groups=mesh['dp'=16,'tensor'=2] {'dp'}, dimensions={1}, use_global_device_ids=true | all-gather | bytes 278528 | tf_op jit(solution)/shard_map/all_gather | solution.py:128
  97.3 5.1 convolution_convert_fusion
  102.4 4.7 copy.64
  115.9 14.6 %while.50 = (s32[]{:T(128)}, bf16[4,8,256,64]{2,3,1,0:T(8,128)(2,1)}, f32[4,8,256]{2,1,0:T(8,128)S(1)}, bf16[4,8,256,64]{2,3,1,0:T(8,128)(2,1)S(1)}, bf16[4,8,25...) while((s32[]{:T(128)}, ...), condition=%wide.region_10.11_spmd.clone, body=%wide.region_5.10_spmd.clone.sunk | while | flops 147880064 | bytes 9204541 | solution.py:165
  136.7 6.9 reduce-scatter.9.cloned.1.call-done
  149.1 43.8 %all-gather.12.cloned.1.call-done = bf16[512,1024]{1,0:T(8,128)(2,1)} async-done(((bf16[32,1024]{1,0:T(8,128)(2,1)}), bf16[512,1024]{1,0:T(8,128)(2,1)}) %all-gather.12.cloned.1.call-update) | async-done | bytes 1048592 | tf_op jit(solution)/shard_map/all_gather | solution.py:129
  192.9 11.4 %all-gather.10.cloned.1.call-done = bf16[2048,512]{1,0:T(8,128)(2,1)} async-done(((bf16[1024,512]{1,0:T(8,128)(2,1)}), bf16[2048,512]{1,0:T(8,128)(2,1)}) %all-gather.10.cloned.1.call-update) | async-done | bytes 2097168 | tf_op jit(solution)/shard_map/all_gather | solution.py:33
  204.3 10.5 %multiply_convert_fusion.2 = (bf16[2048,1024]{1,0:T(8,128)(2,1)}, f32[2048,1024]{1,0:T(8,128)}) fusion(f32[1024]{0:T(1024)S(1)} %copy-done.22, bf16[2048,512]{1,0:T(8,128)(2,1)} %all-gather.10.cloned.1.call-done, bf16[512,1024]{1,0:T(8,128)(2,1)} %all-gather.12.cloned.1.call-done), kind=kOutput, calls=%fused_computation.129 | convolution fusion | flops 2168455168 | bytes 15732736 | tf_op jit(solution)/shard_map/dot_general | solution.py:177
  214.8 49.1 %all-gather.14.cloned.1.call-done = bf16[1024,512]{0,1:T(8,128)(2,1)} async-done(((bf16[1024,32]{0,1:T(8,128)(2,1)}), bf16[1024,512]{0,1:T(8,128)(2,1)}) %all-gather.14.cloned.1.call-update) | async-done | bytes 1048592 | tf_op jit(solution)/shard_map/all_gather | solution.py:130
  263.9 11.0 %all-gather.18.cloned.1.call-done = bf16[1,2048,512]{2,1,0:T(8,128)(2,1)} async-done(((bf16[1,1024,512]{2,1,0:T(8,128)(2,1)}), bf16[1,2048,512]{2,1,0:T(8,128)(2,1)}) %all-gather.18.cloned.1.call-update) | async-done | bytes 2097168 | tf_op jit(solution)/shard_map/all_gather | solution.py:33
  274.9 10.2 %convert_reduce_fusion = (f32[1024]{0:T(1024)S(1)}, bf16[2048,1024]{1,0:T(8,128)(2,1)S(1)}) fusion(f32[2048,1024]{1,0:T(8,128)} %get-tuple-element.587, f32[1024]{0:T(1024)S(1)} %copy-done.22, bf16[1024,512]{0,1:T(8,128)(2,1)} %all-gather.14.cloned.1.call-done, bf16[1,2048,512]{2,1,0:T(8,128)(2,1)} %all-gather.18.cloned.1.call-done), kind=kOutput, calls=%fused_computation.128 | convolution fusion | flops 2195717120 | bytes 15736832 | tf_op jit(solution)/shard_map/sd,fd->sf/dot_general | solution.py:190
  291.1 6.2 convolution_convert_fusion.2
  304.7 10.0 %reduce-scatter.11.cloned.1.call-done = bf16[1024,512]{1,0:T(8,128)(2,1)} async-done(((bf16[2048,512]{1,0:T(8,128)(2,1)}), bf16[1024,512]{1,0:T(8,128)(2,1)}) %reduce-scatter.11.cloned.1.call-update) | async-done | bytes 1048592 | tf_op jit(solution)/shard_map/reduce_scatter | solution.py:37
  319.0 6.6 fusion.131
  325.7 7.2 fusion.155
  341.4 32.6 %while.51 = (s32[]{:T(128)}, bf16[4,8,256,64]{2,3,0,1:T(8,128)(2,1)}, f32[4,8,256,64]{2,3,0,1:T(8,128)}, f32[4,8,256,64]{2,3,0,1:T(8,128)}, f32[4,16,64]{2,1,0:T...) while((s32[]{:T(128)}, ...), condition=%wide.region_21.22_spmd.clone, body=%wide.region_18.21_spmd.clone.sunk | while | flops 361561216 | bytes 22604664 | solution.py:224
  390.9 5.0 convolution_convert_fusion.4
  397.7 17.2 %reduce-scatter.23.cloned.1.call-done = f32[1024,32]{0,1:T(8,128)} async-done(((f32[1024,512]{0,1:T(8,128)}), f32[1024,32]{0,1:T(8,128)}) %reduce-scatter.23.cloned.1.call-update) | async-done | bytes 131088 | tf_op jit(solution)/shard_map/reduce_scatter | solution.py:266
  416.5 78.2 %reduce-scatter.21.cloned.1.call-done = f32[32,1024]{1,0:T(8,128)} async-done(((f32[512,1024]{1,0:T(8,128)}), f32[32,1024]{1,0:T(8,128)}) %reduce-scatter.21.cloned.1.call-update) | async-done | bytes 131088 | tf_op jit(solution)/shard_map/reduce_scatter | solution.py:265
  496.2 74.7 %reduce-scatter.19.cloned.1.call-done = f32[256,32]{0,1:T(8,128)} async-done(((f32[256,512]{0,1:T(8,128)}), f32[256,32]{0,1:T(8,128)}) %reduce-scatter.19.cloned.1.call-update) | async-done | bytes 32784 | tf_op jit(solution)/shard_map/reduce_scatter | solution.py:264
  572.3 76.1 %reduce-scatter.17.cloned.1.call-done = f32[32,3,256]{2,0,1:T(8,128)} async-done(((f32[512,3,256]{2,0,1:T(8,128)}), f32[32,3,256]{2,0,1:T(8,128)}) %reduce-scatter.17.cloned.1.call-update) | async-done | bytes 98320 | tf_op jit(solution)/shard_map/reduce_scatter | solution.py:263
  650.0 7.2 reduce-scatter.15.cloned.1.call-done
  663.2 77.1 %all-reduce = (f32[512]{0:T(512)S(1)}, f32[512]{0:T(512)S(1)}, f32[512]{0:T(512)S(1)}, f32[2048]{0:T(1024)S(1)}, f32[512]{0:T(512)S(1)}) all-reduce(f32[512]{0:T(512)S(1)} %get-tuple-element.562, f32[512]{0:T(512)S(1)} %get-tuple-element.563, f32[512]{0:T(512)S(1)} %get-tuple-element.564, ...), channel_id=1, replica_groups=mesh['dp'=16,'tensor'=2] {'dp'}, use_global_device_ids=true, to_apply=%region_27.28 | all-reduce | flops 4096 | bytes 32768 | tf_op jit(solution)/shard_map/psum | solution.py:261
  (259 shorter events, 136.5 us)
Async XLA Ops:
  8.0 89.3 %all-gather.8.cloned.1.call-start = ((), (), s32[]{:S(2)}) async-start(), calls=%async_computation.8 | async-start | bytes 3145728 | tf_op jit(solution)/shard_map/all_gather | solution.py:33
  12.8 47.6 %copy-start.18 = (bf16[256,32]{0,1:T(8,128)(2,1)S(1)}, bf16[256,32]{0,1:T(8,128)(2,1)}, u32[]{:S(2)}) copy-start(bf16[256,32]{0,1:T(8,128)(2,1)} %param.23) | copy-start | bytes 49156
  12.8 130.9 %reduce-scatter.9.cloned.1.call-start = ((), (), s32[]{:S(2)}) async-start(), calls=%async_computation.9 | async-start | bytes 3145728 | tf_op jit(solution)/shard_map/reduce_scatter | solution.py:37
  60.4 42.1 %copy-start.10 = (bf16[512,3,256]{0,2,1:T(8,128)(2,1)}, bf16[512,3,256]{0,2,1:T(8,128)(2,1)S(1)}, u32[]{:S(2)}) copy-start(bf16[512,3,256]{0,2,1:T(8,128)(2,1)S(1)} %copy.63) | copy-start | bytes 2359300
  133.9 9.7 %copy-start.13 = (f32[512]{0:T(512)S(1)}, f32[512]{0:T(512)}, u32[]{:S(2)}) copy-start(f32[512]{0:T(512)} %param.24) | copy-start | bytes 6148
  136.1 56.8 %all-gather.12.cloned.1.call-start = ((), (), s32[]{:S(2)}) async-start(), calls=%async_computation.11 | async-start | bytes 1114112 | tf_op jit(solution)/shard_map/all_gather | solution.py:129
  136.7 9.4 %copy-start.17 = (f32[512]{0:T(512)S(1)}, f32[512]{0:T(512)}, u32[]{:S(2)}) copy-start(f32[512]{0:T(512)} %param.25) | copy-start | bytes 6148
  136.7 67.6 %all-gather.10.cloned.1.call-start = ((), (), s32[]{:S(2)}) async-start(), calls=%async_computation.10 | async-start | bytes 3145728 | tf_op jit(solution)/shard_map/all_gather | solution.py:33
  146.1 58.2 %copy-start.22 = (f32[1024]{0:T(1024)S(1)}, f32[1024]{0:T(1024)}, u32[]{:S(2)}) copy-start(f32[1024]{0:T(1024)} %param.27) | copy-start | bytes 12292
  147.6 116.3 %all-gather.14.cloned.1.call-start = ((), (), s32[]{:S(2)}) async-start(), calls=%async_computation.12 | async-start | bytes 1114112 | tf_op jit(solution)/shard_map/all_gather | solution.py:130
  148.2 126.7 %all-gather.18.cloned.1.call-start = ((), (), s32[]{:S(2)}) async-start(), calls=%async_computation.21 | async-start | bytes 3145728 | tf_op jit(solution)/shard_map/all_gather | solution.py:33
  148.9 152.9 %reduce-scatter.13.cloned.1.call-start = ((), (), s32[]{:S(2)}) async-start(), calls=%async_computation.14 | async-start | bytes 3145728 | tf_op jit(solution)/shard_map/reduce_scatter | solution.py:37
  274.9 12.1 %copy-start.21 = (bf16[512,1024]{1,0:T(8,128)(2,1)S(1)}, bf16[512,1024]{1,0:T(8,128)(2,1)}, u32[]{:S(2)}) copy-start(bf16[512,1024]{1,0:T(8,128)(2,1)} %all-gather.12.cloned.1.call-done) | copy-start | bytes 3145732
  290.9 23.9 %reduce-scatter.11.cloned.1.call-start = ((), (), s32[]{:S(2)}) async-start(), calls=%async_computation.13 | async-start | bytes 3145728 | tf_op jit(solution)/shard_map/reduce_scatter | solution.py:37
  297.3 17.4 %copy-start.19 = (f32[512]{0:T(512)S(1)}, f32[512]{0:T(512)}, u32[]{:S(2)}) copy-start(f32[512]{0:T(512)} %param.29) | copy-start | bytes 6148
  297.4 35.9 %all-gather.16.cloned.1.call-start = ((), (), s32[]{:S(2)}) async-start(), calls=%async_computation.15 | async-start | bytes 3145728 | tf_op jit(solution)/shard_map/all_gather | solution.py:33
  318.9 95.9 %reduce-scatter.23.cloned.1.call-start = ((), (), s32[]{:S(2)}) async-start(), calls=%async_computation.20 | async-start | bytes 2228224 | tf_op jit(solution)/shard_map/reduce_scatter | solution.py:266
  325.6 169.1 %reduce-scatter.21.cloned.1.call-start = ((), (), s32[]{:S(2)}) async-start(), calls=%async_computation.19 | async-start | bytes 2228224 | tf_op jit(solution)/shard_map/reduce_scatter | solution.py:265
  332.9 238.1 %reduce-scatter.19.cloned.1.call-start = ((), (), s32[]{:S(2)}) async-start(), calls=%async_computation.18 | async-start | bytes 557056 | tf_op jit(solution)/shard_map/reduce_scatter | solution.py:264
  336.5 4.9 copy-start.15
  336.5 4.9 copy-start.24
  377.7 270.8 %reduce-scatter.17.cloned.1.call-start = ((), (), s32[]{:S(2)}) async-start(), calls=%async_computation.17 | async-start | bytes 1671168 | tf_op jit(solution)/shard_map/reduce_scatter | solution.py:263
  390.6 266.6 %reduce-scatter.15.cloned.1.call-start = ((), (), s32[]{:S(2)}) async-start(), calls=%async_computation.16 | async-start | bytes 3145728 | tf_op jit(solution)/shard_map/reduce_scatter | solution.py:37
  657.2 86.0 %copy-start.6 = (bf16[1024,512]{1,0:T(8,128)(2,1)S(1)}, bf16[1024,512]{1,0:T(8,128)(2,1)}, u32[]{:S(2)}) copy-start(bf16[1024,512]{1,0:T(8,128)(2,1)} %reduce-scatter.15.cloned.1.call-done) | copy-start | bytes 3145732
  (16 other events, 40.4 us)
Sparse Core Ops, SparseCore 0:
  12.9 13.2 all-gather.7
  136.2 7.4 reduce-scatter.8
  291.0 10.8 reduce-scatter.12
  303.9 10.7 reduce-scatter.10
Sparse Core Ops, SparseCore 1:
  139.7 53.1 all-gather.11
  195.0 9.3 all-gather.9
  207.3 56.5 all-gather.13
  265.6 9.3 all-gather.17
  319.0 11.6 all-gather.15
  333.1 81.7 reduce-scatter.22
  417.1 77.5 reduce-scatter.20
  497.4 73.5 reduce-scatter.18
  573.1 75.3 reduce-scatter.16
  650.8 6.3 reduce-scatter.14
